TPU v7x, 512 devices: a whole 4x8x8 slice. The times are simulated.
512 devices in a mesh: gx: 64 (over y, z_lo, core), gy: 8 (over z_hi, x).
Axes of the slice: x: 4, y: 8, z: 8 (z_hi: 2, z_lo: 4; z = z_hi * 4 + z_lo), core: 2. Of those that a mesh axis runs over, the one named last changes fastest.
Arguments:
- pops: float32 [19, 256, 64, 128], P(None, 'gx', 'gy'), may hold values from 0.005 to 0.5, as said below
- label: int32 [256, 64, 128], P('gx', 'gy'), may hold values from 0 to 2, as said below
- drive: float32 [3, 256, 64, 128], P(None, 'gx', 'gy'), may hold values from -0.3 to 0.3
Outputs:
- momentum: float32 [3, 256, 64, 128], P(None, 'gx', 'gy')
- running: float32 [3, 64, 16, 32], P(None, 'gx', 'gy')
Inputs may be any that keep to these rules, and one draw needn't show every extreme that they name: `pops`: populations near a local equilibrium with density 0.8 to 1.2 and each velocity component within 0.1. `label`: 2 marks walls: every cell with z index 0 or 127, and scattered obstacle cells; elsewhere 1 marks the second solution, 0 the first.
All inputs are finite; a program needn't handle non-finite values.
Results may differ from a plain program's by a relative error of at most 0.0003.
Values sent between devices are 32-bit elements; how exact they have to be, the bound alone decides.
No kernel may reach another device: no remote copies, remote signals or barrier semaphores. Data moves between devices by JAX's collectives and lax.ppermute only.
A program may use at most 64 MiB of HBM per device.

v0:
```python
import math
import jax
import jax.numpy as jnp
from jax import lax
from jax.sharding import PartitionSpec as P

NZ = 128
STEPS = 4
VELOCITY = [
    [0, 0, 0],
    [1, 0, 0],
    [-1, 0, 0],
    [0, 1, 0],
    [0, -1, 0],
    [0, 0, 1],
    [0, 0, -1],
    [1, 1, 0],
    [-1, -1, 0],
    [1, -1, 0],
    [-1, 1, 0],
    [1, 0, 1],
    [-1, 0, -1],
    [1, 0, -1],
    [-1, 0, 1],
    [0, 1, 1],
    [0, -1, -1],
    [0, 1, -1],
    [0, -1, 1],
]
OPPOSITE = [0, 2, 1, 4, 3, 6, 5, 8, 7, 10, 9, 12, 11, 14, 13, 16, 15, 18, 17]
WEIGHTS = [1.0 / 3.0] + [1.0 / 18.0] * 6 + [1.0 / 36.0] * 12
PAIRS = [(0, 0), (1, 1), (2, 2), (0, 1), (0, 2), (1, 2)]
COMPONENT = [[0, 3, 4], [3, 1, 5], [4, 5, 2]]
SLOW_VISCOSITY = 0.0004


def with_halo(cells, sides, width):
    for axis, dim in sides:
        count = lax.axis_size(axis)
        head = lax.slice_in_dim(cells, 0, width, axis=dim)
        tail = lax.slice_in_dim(cells, cells.shape[dim] - width, cells.shape[dim], axis=dim)
        cells = jnp.concatenate(
            [
                lax.ppermute(tail, axis, [(i, (i + 1) % count) for i in range(count)]),
                cells,
                lax.ppermute(head, axis, [((i + 1) % count, i) for i in range(count)]),
            ],
            axis=dim,
        )
    return cells


def collide(pops, label, drive, phase):
    columns = [
        jnp.array([row[axis_id] for row in VELOCITY], jnp.float32).reshape(19, 1, 1, 1)
        for axis_id in range(3)
    ]
    weights = jnp.array(WEIGHTS, jnp.float32).reshape(19, 1, 1, 1)
    density = jnp.sum(pops, axis=0)
    moment = [jnp.sum(columns[axis_id] * pops, axis=0) for axis_id in range(3)]
    speed = [moment[axis_id] / density for axis_id in range(3)]
    along = columns[0] * speed[0] + columns[1] * speed[1] + columns[2] * speed[2]
    square = speed[0] * speed[0] + speed[1] * speed[1] + speed[2] * speed[2]
    balance = weights * density * (1.0 + 3.0 * along + 4.5 * along * along - 1.5 * square)
    second = label == 1
    solid = label == 2
    omega = jnp.where(second, 1.1, 1.6)
    strength = jnp.where(second, 0.6, 1.0) * phase
    push = columns[0] * drive[0] + columns[1] * drive[1] + columns[2] * drive[2]
    relaxed = pops - omega * (pops - balance) + 3.0 * weights * strength * push
    bounced = jnp.stack([pops[other] for other in OPPOSITE])
    post = jnp.where(solid, bounced, relaxed)
    fluid = jnp.where(solid, 0.0, 1.0)
    stress = jnp.stack([moment[first] * moment[later] / density * fluid for first, later in PAIRS])
    return (post, stress)


def momentum_of(pops):
    columns = [
        jnp.array([row[axis_id] for row in VELOCITY], jnp.float32).reshape(19, 1, 1, 1)
        for axis_id in range(3)
    ]
    return jnp.stack([jnp.sum(columns[axis_id] * pops, axis=0) for axis_id in range(3)])


def tables(length):
    index = jnp.arange(length, dtype=jnp.int32)
    turns = index[:, None] * index[None, :] % length
    angle = turns.astype(jnp.float32) * (2.0 * math.pi / length)
    return (jnp.cos(angle), jnp.sin(angle))


def product(values, table):
    return jnp.matmul(values, table, precision=lax.Precision.HIGHEST)


def transform(real, imag, axis_id, inverse):
    length = real.shape[axis_id]
    cosine, sine = tables(length)
    real_last = jnp.moveaxis(real, axis_id, -1)
    imag_last = jnp.moveaxis(imag, axis_id, -1)
    if inverse:
        out_real = (product(real_last, cosine) - product(imag_last, sine)) / length
        out_imag = (product(imag_last, cosine) + product(real_last, sine)) / length
    else:
        out_real = product(real_last, cosine) + product(imag_last, sine)
        out_imag = product(imag_last, cosine) - product(real_last, sine)
    return (jnp.moveaxis(out_real, -1, axis_id), jnp.moveaxis(out_imag, -1, axis_id))


def wavenumber(index, length):
    shifted = index - length * (index >= (length + 1) // 2).astype(jnp.int32)
    return shifted.astype(jnp.float32) * (2.0 * math.pi / length)


def local(pops, label, drive):
    width = pops.shape[1]
    height = pops.shape[2]
    state = pops
    total = jnp.zeros((6,) + pops.shape[1:], jnp.float32)
    for step in range(STEPS):
        phase = math.cos(2.0 * math.pi * (step + 0.5) / STEPS)
        post, stress = collide(state, label, drive, phase)
        total = total + stress
        padded = with_halo(post, (("gx", 1), ("gy", 2)), 1)
        moved = []
        for index in range(19):
            start_x = 1 - VELOCITY[index][0]
            start_y = 1 - VELOCITY[index][1]
            piece = padded[index, start_x : start_x + width, start_y : start_y + height, :]
            moved.append(jnp.roll(piece, VELOCITY[index][2], axis=2))
        state = jnp.stack(moved)
    momentum = momentum_of(state)
    block_x = width // 4
    block_y = height // 4
    slow_z = NZ // 4
    slow = (total / STEPS).reshape(6, block_x, 4, block_y, 4, slow_z, 4).mean(axis=(2, 4, 6))
    cosine_z, sine_z = tables(slow_z)
    spectrum = jnp.stack([product(slow, cosine_z), -product(slow, sine_z)])
    spectrum = lax.all_to_all(spectrum, "gy", split_axis=4, concat_axis=3, tiled=True)
    full_y = spectrum.shape[3]
    part_z = spectrum.shape[4]
    real, imag = transform(spectrum[0], spectrum[1], 2, False)
    spectrum = jnp.stack([real, imag]).reshape(2, 6, block_x, full_y * part_z)
    spectrum = lax.all_to_all(spectrum, "gx", split_axis=3, concat_axis=2, tiled=True)
    full_x = spectrum.shape[2]
    part_m = spectrum.shape[3]
    real, imag = transform(spectrum[0], spectrum[1], 1, False)
    wave_x = wavenumber(jnp.arange(full_x, dtype=jnp.int32), full_x).reshape(full_x, 1)
    flat = lax.axis_index("gx") * part_m + jnp.arange(part_m, dtype=jnp.int32)
    row_y = flat // part_z
    index_z = lax.axis_index("gy") * part_z + flat % part_z
    wave_y = wavenumber(row_y, full_y).reshape(1, part_m)
    wave_z = wavenumber(index_z, slow_z).reshape(1, part_m)
    waves = [wave_x, wave_y, wave_z]
    force_real = [
        waves[0] * imag[COMPONENT[first][0]]
        + waves[1] * imag[COMPONENT[first][1]]
        + waves[2] * imag[COMPONENT[first][2]]
        for first in range(3)
    ]
    force_imag = [
        -(
            waves[0] * real[COMPONENT[first][0]]
            + waves[1] * real[COMPONENT[first][1]]
            + waves[2] * real[COMPONENT[first][2]]
        )
        for first in range(3)
    ]
    wave_sq = wave_x * wave_x + wave_y * wave_y + wave_z * wave_z
    positive = wave_sq > 0
    safe = jnp.where(positive, wave_sq, 1.0)
    inner_real = waves[0] * force_real[0] + waves[1] * force_real[1] + waves[2] * force_real[2]
    inner_imag = waves[0] * force_imag[0] + waves[1] * force_imag[1] + waves[2] * force_imag[2]
    speed_real = jnp.stack(
        [
            jnp.where(
                positive,
                (force_real[first] - waves[first] * inner_real / safe) / (SLOW_VISCOSITY * safe),
                0.0,
            )
            for first in range(3)
        ]
    )
    speed_imag = jnp.stack(
        [
            jnp.where(
                positive,
                (force_imag[first] - waves[first] * inner_imag / safe) / (SLOW_VISCOSITY * safe),
                0.0,
            )
            for first in range(3)
        ]
    )
    real, imag = transform(speed_real, speed_imag, 1, True)
    result = lax.all_to_all(jnp.stack([real, imag]), "gx", split_axis=2, concat_axis=3, tiled=True)
    result = result.reshape(2, 3, block_x, full_y, part_z)
    real, imag = transform(result[0], result[1], 2, True)
    result = lax.all_to_all(jnp.stack([real, imag]), "gy", split_axis=3, concat_axis=4, tiled=True)
    running = (product(result[0], cosine_z) - product(result[1], sine_z)) / slow_z
    return (momentum, running)


def solution(mesh):
    in_specs = (P(None, "gx", "gy", None), P("gx", "gy", None), P(None, "gx", "gy", None))
    out_specs = (P(None, "gx", "gy", None), P(None, "gx", "gy", None))
    return jax.shard_map(local, mesh=mesh, in_specs=in_specs, out_specs=out_specs, check_vma=False)
```

profile of v0, /device:TPU:6, one launch (start us, length us, event | category | flops | bytes accessed | tf_op | source)
XLA Modules:
  0.0 232.1 jit_solution(13145048456317366882)
XLA Ops:
  11.3 10.2 %collective-permute-start = (f32[19,1,8,128]{3,2,1,0:T(8,128)S(1)}, f32[19,1,8,128]{3,2,1,0:T(8,128)S(1)}, u32[]{:S(2)}, u32[]{:S(2)}) collective-permute-start(f32[19,1,8,128]{3,2,1,0:T(8,128)S(1)} %get-tuple-element.234), channel_id=1, source_target_pairs={{8,0},{16,8},{24,16},{32,24},{40,32},{48,40},{56,48},{64,56},{72,6... | collective-permute-start | bytes 233480 | tf_op jit(solution)/shard_map/ppermute | solution.py:46
  21.5 1.9 collective-permute-start.1
  28.6 2.6 %collective-permute-done.1 = f32[19,1,8,128]{3,2,1,0:T(8,128)S(1)} collective-permute-done((f32[19,1,8,128]{3,2,1,0:T(8,128)S(1)}, f32[19,1,8,128]{3,2,1,0:T(8,128)S(1)}, u32[]{:S(2)}, u32[]{:S(2)}) %collective-permute-start.1) | collective-permute-done | bytes 77856 | tf_op jit(solution)/shard_map/ppermute | solution.py:44
  31.2 8.1 %collective-permute-start.3 = (f32[19,6,1,128]{3,2,1,0:T(1,128)S(1)}, f32[19,6,1,128]{3,2,1,0:T(1,128)S(1)}, u32[]{:S(2)}, u32[]{:S(2)}) collective-permute-start(f32[19,6,1,128]{3,2,1,0:T(1,128)S(1)} %get-tuple-element.202), channel_id=1, source_target_pairs={{0,1},{1,2},{2,3},{3,4},{4,5},{5,6},{6,7},{7,0},{8,9},{9,10},{10,1... | collective-permute-start | bytes 175112 | tf_op jit(solution)/shard_map/ppermute | solution.py:44
  39.4 1.9 collective-permute-start.2
  41.5 9.9 %collective-permute-done.2 = f32[19,6,1,128]{3,2,1,0:T(1,128)S(1)} collective-permute-done((f32[19,6,1,128]{3,2,1,0:T(1,128)S(1)}, f32[19,6,1,128]{3,2,1,0:T(1,128)S(1)}, u32[]{:S(2)}, u32[]{:S(2)}) %collective-permute-start.2) | collective-permute-done | bytes 58400 | tf_op jit(solution)/shard_map/ppermute | solution.py:46
  53.8 3.5 %collective-permute-start.4 = (f32[19,1,8,128]{3,2,1,0:T(8,128)S(1)}, f32[19,1,8,128]{3,2,1,0:T(8,128)S(1)}, u32[]{:S(2)}, u32[]{:S(2)}) collective-permute-start(f32[19,1,8,128]{3,2,1,0:T(8,128)S(1)} %get-tuple-element.230), channel_id=1, source_target_pairs={{8,0},{16,8},{24,16},{32,24},{40,32},{48,40},{56,48},{64,56},{72,6... | collective-permute-start | bytes 233480 | tf_op jit(solution)/shard_map/ppermute | solution.py:46
  57.3 1.9 collective-permute-start.5
  60.1 7.0 %collective-permute-done.5 = f32[19,1,8,128]{3,2,1,0:T(8,128)S(1)} collective-permute-done((f32[19,1,8,128]{3,2,1,0:T(8,128)S(1)}, f32[19,1,8,128]{3,2,1,0:T(8,128)S(1)}, u32[]{:S(2)}, u32[]{:S(2)}) %collective-permute-start.5) | collective-permute-done | bytes 77856 | tf_op jit(solution)/shard_map/ppermute | solution.py:44
  67.1 1.9 collective-permute-start.7
  69.1 3.9 %collective-permute-start.6 = (f32[19,6,1,128]{3,2,1,0:T(1,128)S(1)}, f32[19,6,1,128]{3,2,1,0:T(1,128)S(1)}, u32[]{:S(2)}, u32[]{:S(2)}) collective-permute-start(f32[19,6,1,128]{3,2,1,0:T(1,128)S(1)} %get-tuple-element.199), channel_id=1, source_target_pairs={{1,0},{2,1},{3,2},{4,3},{5,4},{6,5},{7,6},{0,7},{9,8},{10,9},{11,1... | collective-permute-start | bytes 175112 | tf_op jit(solution)/shard_map/ppermute | solution.py:46
  73.4 7.8 %collective-permute-done.6 = f32[19,6,1,128]{3,2,1,0:T(1,128)S(1)} collective-permute-done((f32[19,6,1,128]{3,2,1,0:T(1,128)S(1)}, f32[19,6,1,128]{3,2,1,0:T(1,128)S(1)}, u32[]{:S(2)}, u32[]{:S(2)}) %collective-permute-start.6) | collective-permute-done | bytes 58400 | tf_op jit(solution)/shard_map/ppermute | solution.py:46
  83.4 1.9 collective-permute-start.8
  85.4 2.4 %collective-permute-start.9 = (f32[19,1,8,128]{3,2,1,0:T(8,128)S(1)}, f32[19,1,8,128]{3,2,1,0:T(8,128)S(1)}, u32[]{:S(2)}, u32[]{:S(2)}) collective-permute-start(f32[19,1,8,128]{3,2,1,0:T(8,128)S(1)} %get-tuple-element.227), channel_id=1, source_target_pairs={{0,8},{8,16},{16,24},{24,32},{32,40},{40,48},{48,56},{56,64},{64,7... | collective-permute-start | bytes 233480 | tf_op jit(solution)/shard_map/ppermute | solution.py:44
  88.6 6.4 %collective-permute-done.9 = f32[19,1,8,128]{3,2,1,0:T(8,128)S(1)} collective-permute-done((f32[19,1,8,128]{3,2,1,0:T(8,128)S(1)}, f32[19,1,8,128]{3,2,1,0:T(8,128)S(1)}, u32[]{:S(2)}, u32[]{:S(2)}) %collective-permute-start.9) | collective-permute-done | bytes 77856 | tf_op jit(solution)/shard_map/ppermute | solution.py:44
  95.1 1.9 collective-permute-start.11
  97.0 4.1 %collective-permute-start.10 = (f32[19,6,1,128]{3,2,1,0:T(1,128)S(1)}, f32[19,6,1,128]{3,2,1,0:T(1,128)S(1)}, u32[]{:S(2)}, u32[]{:S(2)}) collective-permute-start(f32[19,6,1,128]{3,2,1,0:T(1,128)S(1)} %get-tuple-element.197), channel_id=1, source_target_pairs={{1,0},{2,1},{3,2},{4,3},{5,4},{6,5},{7,6},{0,7},{9,8},{10,9},{11,1... | collective-permute-start | bytes 175112 | tf_op jit(solution)/shard_map/ppermute | solution.py:46
  101.3 7.8 %collective-permute-done.10 = f32[19,6,1,128]{3,2,1,0:T(1,128)S(1)} collective-permute-done((f32[19,6,1,128]{3,2,1,0:T(1,128)S(1)}, f32[19,6,1,128]{3,2,1,0:T(1,128)S(1)}, u32[]{:S(2)}, u32[]{:S(2)}) %collective-permute-start.10) | collective-permute-done | bytes 58400 | tf_op jit(solution)/shard_map/ppermute | solution.py:46
  141.7 4.8 %all-to-all-start = ((f32[2,6,1,2,32]{1,3,2,0,4:T(2,128)}), f32[2,6,1,2,32]{1,3,2,0,4:T(2,128)S(1)}, u32[]{:S(2)}, u32[]{:S(2)}) async-start(f32[2,6,1,2,32]{1,3,2,0,4:T(2,128)} %copy.171), calls=%async_computation | async-start | bytes 131072 | tf_op jit(solution)/shard_map/all_to_all | solution.py:140
  146.6 8.2 %all-to-all-done = f32[2,6,1,2,32]{1,3,2,0,4:T(2,128)S(1)} async-done(((f32[2,6,1,2,32]{1,3,2,0,4:T(2,128)}), f32[2,6,1,2,32]{1,3,2,0,4:T(2,128)S(1)}, u32[]{:S(2)}, u32[]{:S(2)}) %all-to-all-start) | async-done | bytes 3104 | tf_op jit(solution)/shard_map/all_to_all | solution.py:140
  157.8 5.6 %all-to-all-start.1 = ((f32[2,6,1,64]{1,0,2,3:T(2,128)}), f32[2,6,1,64]{1,0,2,3:T(2,128)S(1)}, u32[]{:S(2)}, u32[]{:S(2)}) async-start(f32[2,6,1,64]{1,0,2,3:T(2,128)} %copy.179), calls=%async_computation.1 | async-start | bytes 131072 | tf_op jit(solution)/shard_map/all_to_all | solution.py:145
  164.5 8.8 %all-to-all-done.1 = f32[2,6,1,64]{1,0,2,3:T(2,128)S(1)} async-done(((f32[2,6,1,64]{1,0,2,3:T(2,128)}), f32[2,6,1,64]{1,0,2,3:T(2,128)S(1)}, u32[]{:S(2)}, u32[]{:S(2)}) %all-to-all-start.1) | async-done | bytes 3104 | tf_op jit(solution)/shard_map/all_to_all | solution.py:145
  176.5 4.6 %all-to-all-start.2 = ((f32[2,3,64,1]{1,3,0,2:T(1,128)}), f32[2,3,64,1]{1,3,0,2:T(1,128)S(1)}, u32[]{:S(2)}, u32[]{:S(2)}) async-start(f32[2,3,64,1]{1,3,0,2:T(1,128)} %copy.182), calls=%async_computation.2 | async-start | bytes 131072 | tf_op jit(solution)/shard_map/all_to_all | solution.py:196
  181.1 10.0 %all-to-all-done.2 = f32[2,3,64,1]{1,3,0,2:T(1,128)S(1)} async-done(((f32[2,3,64,1]{1,3,0,2:T(1,128)}), f32[2,3,64,1]{1,3,0,2:T(1,128)S(1)}, u32[]{:S(2)}, u32[]{:S(2)}) %all-to-all-start.2) | async-done | bytes 1568 | tf_op jit(solution)/shard_map/all_to_all | solution.py:196
  193.0 5.3 %all-to-all-start.3 = ((f32[2,3,1,16,4]{4,0,2,1,3:T(2,128)}), f32[2,3,1,16,4]{4,0,2,1,3:T(2,128)S(1)}, u32[]{:S(2)}, u32[]{:S(2)}) async-start(f32[2,3,1,16,4]{4,0,2,1,3:T(2,128)} %copy.187), calls=%async_computation.3 | async-start | bytes 98304 | tf_op jit(solution)/shard_map/all_to_all | solution.py:199
  198.3 2.3 %collective-permute-start.13 = (f32[19,1,8,128]{3,2,1,0:T(8,128)S(1)}, f32[19,1,8,128]{3,2,1,0:T(8,128)S(1)}, u32[]{:S(2)}, u32[]{:S(2)}) collective-permute-start(f32[19,1,8,128]{3,2,1,0:T(8,128)S(1)} %get-tuple-element.222), channel_id=1, source_target_pairs={{8,0},{16,8},{24,16},{32,24},{40,32},{48,40},{56,48},{64,56},{72,6... | collective-permute-start | bytes 233480 | tf_op jit(solution)/shard_map/ppermute | solution.py:46
  200.7 2.0 collective-permute-start.12
  202.7 3.8 %all-to-all-done.3 = f32[2,3,1,16,4]{4,0,2,1,3:T(2,128)S(1)} async-done(((f32[2,3,1,16,4]{4,0,2,1,3:T(2,128)}), f32[2,3,1,16,4]{4,0,2,1,3:T(2,128)S(1)}, u32[]{:S(2)}, u32[]{:S(2)}) %all-to-all-start.3) | async-done | bytes 1568 | tf_op jit(solution)/shard_map/all_to_all | solution.py:199
  207.8 2.5 %collective-permute-done.12 = f32[19,1,8,128]{3,2,1,0:T(8,128)S(1)} collective-permute-done((f32[19,1,8,128]{3,2,1,0:T(8,128)S(1)}, f32[19,1,8,128]{3,2,1,0:T(8,128)S(1)}, u32[]{:S(2)}, u32[]{:S(2)}) %collective-permute-start.12) | collective-permute-done | bytes 77856 | tf_op jit(solution)/shard_map/ppermute | solution.py:44
  210.4 7.3 %collective-permute-start.14 = (f32[19,6,1,128]{3,2,1,0:T(1,128)S(1)}, f32[19,6,1,128]{3,2,1,0:T(1,128)S(1)}, u32[]{:S(2)}, u32[]{:S(2)}) collective-permute-start(f32[19,6,1,128]{3,2,1,0:T(1,128)S(1)} %get-tuple-element.196), channel_id=1, source_target_pairs={{0,1},{1,2},{2,3},{3,4},{4,5},{5,6},{6,7},{7,0},{8,9},{9,10},{10,1... | collective-permute-start | bytes 175112 | tf_op jit(solution)/shard_map/ppermute | solution.py:44
  217.7 1.9 collective-permute-start.15
  219.6 10.1 %collective-permute-done.15 = f32[19,6,1,128]{3,2,1,0:T(1,128)S(1)} collective-permute-done((f32[19,6,1,128]{3,2,1,0:T(1,128)S(1)}, f32[19,6,1,128]{3,2,1,0:T(1,128)S(1)}, u32[]{:S(2)}, u32[]{:S(2)}) %collective-permute-start.15) | collective-permute-done | bytes 58400 | tf_op jit(solution)/shard_map/ppermute | solution.py:46
  (434 shorter events, 67.0 us)
Async XLA Ops:
  0.6 7.3 %copy-start = (f32[19,4,8,128]{3,2,1,0:T(8,128)S(1)}, f32[19,4,8,128]{3,2,1,0:T(8,128)}, u32[]{:S(2)}) copy-start(f32[19,4,8,128]{3,2,1,0:T(8,128)} %param.22) | copy-start | bytes 933892
  10.2 1.1 copy-start.19
  11.3 17.2 %collective-permute-start = (f32[19,1,8,128]{3,2,1,0:T(8,128)S(1)}, f32[19,1,8,128]{3,2,1,0:T(8,128)S(1)}, u32[]{:S(2)}, u32[]{:S(2)}) collective-permute-start(f32[19,1,8,128]{3,2,1,0:T(8,128)S(1)} %get-tuple-element.234), channel_id=1, source_target_pairs={{8,0},{16,8},{24,16},{32,24},{40,32},{48,40},{56,48},{64,56},{72,6... | collective-permute-start | bytes 233480 | tf_op jit(solution)/shard_map/ppermute | solution.py:46
  21.5 9.6 %collective-permute-start.1 = (f32[19,1,8,128]{3,2,1,0:T(8,128)S(1)}, f32[19,1,8,128]{3,2,1,0:T(8,128)S(1)}, u32[]{:S(2)}, u32[]{:S(2)}) collective-permute-start(f32[19,1,8,128]{3,2,1,0:T(8,128)S(1)} %get-tuple-element.235), channel_id=1, source_target_pairs={{0,8},{8,16},{16,24},{24,32},{32,40},{40,48},{48,56},{56,64},{64,7... | collective-permute-start | bytes 233480 | tf_op jit(solution)/shard_map/ppermute | solution.py:44
  31.2 10.1 %collective-permute-start.3 = (f32[19,6,1,128]{3,2,1,0:T(1,128)S(1)}, f32[19,6,1,128]{3,2,1,0:T(1,128)S(1)}, u32[]{:S(2)}, u32[]{:S(2)}) collective-permute-start(f32[19,6,1,128]{3,2,1,0:T(1,128)S(1)} %get-tuple-element.202), channel_id=1, source_target_pairs={{0,1},{1,2},{2,3},{3,4},{4,5},{5,6},{6,7},{7,0},{8,9},{9,10},{10,1... | collective-permute-start | bytes 175112 | tf_op jit(solution)/shard_map/ppermute | solution.py:44
  39.4 12.1 %collective-permute-start.2 = (f32[19,6,1,128]{3,2,1,0:T(1,128)S(1)}, f32[19,6,1,128]{3,2,1,0:T(1,128)S(1)}, u32[]{:S(2)}, u32[]{:S(2)}) collective-permute-start(f32[19,6,1,128]{3,2,1,0:T(1,128)S(1)} %get-tuple-element.201), channel_id=1, source_target_pairs={{1,0},{2,1},{3,2},{4,3},{5,4},{6,5},{7,6},{0,7},{9,8},{10,9},{11,1... | collective-permute-start | bytes 175112 | tf_op jit(solution)/shard_map/ppermute | solution.py:46
  53.8 6.3 %collective-permute-start.4 = (f32[19,1,8,128]{3,2,1,0:T(8,128)S(1)}, f32[19,1,8,128]{3,2,1,0:T(8,128)S(1)}, u32[]{:S(2)}, u32[]{:S(2)}) collective-permute-start(f32[19,1,8,128]{3,2,1,0:T(8,128)S(1)} %get-tuple-element.230), channel_id=1, source_target_pairs={{8,0},{16,8},{24,16},{32,24},{40,32},{48,40},{56,48},{64,56},{72,6... | collective-permute-start | bytes 233480 | tf_op jit(solution)/shard_map/ppermute | solution.py:46
  57.3 9.8 %collective-permute-start.5 = (f32[19,1,8,128]{3,2,1,0:T(8,128)S(1)}, f32[19,1,8,128]{3,2,1,0:T(8,128)S(1)}, u32[]{:S(2)}, u32[]{:S(2)}) collective-permute-start(f32[19,1,8,128]{3,2,1,0:T(8,128)S(1)} %get-tuple-element.231), channel_id=1, source_target_pairs={{0,8},{8,16},{16,24},{24,32},{32,40},{40,48},{48,56},{56,64},{64,7... | collective-permute-start | bytes 233480 | tf_op jit(solution)/shard_map/ppermute | solution.py:44
  67.1 6.1 %collective-permute-start.7 = (f32[19,6,1,128]{3,2,1,0:T(1,128)S(1)}, f32[19,6,1,128]{3,2,1,0:T(1,128)S(1)}, u32[]{:S(2)}, u32[]{:S(2)}) collective-permute-start(f32[19,6,1,128]{3,2,1,0:T(1,128)S(1)} %get-tuple-element.200), channel_id=1, source_target_pairs={{0,1},{1,2},{2,3},{3,4},{4,5},{5,6},{6,7},{7,0},{8,9},{9,10},{10,1... | collective-permute-start | bytes 175112 | tf_op jit(solution)/shard_map/ppermute | solution.py:44
  69.1 12.1 %collective-permute-start.6 = (f32[19,6,1,128]{3,2,1,0:T(1,128)S(1)}, f32[19,6,1,128]{3,2,1,0:T(1,128)S(1)}, u32[]{:S(2)}, u32[]{:S(2)}) collective-permute-start(f32[19,6,1,128]{3,2,1,0:T(1,128)S(1)} %get-tuple-element.199), channel_id=1, source_target_pairs={{1,0},{2,1},{3,2},{4,3},{5,4},{6,5},{7,6},{0,7},{9,8},{10,9},{11,1... | collective-permute-start | bytes 175112 | tf_op jit(solution)/shard_map/ppermute | solution.py:46
  83.4 5.2 %collective-permute-start.8 = (f32[19,1,8,128]{3,2,1,0:T(8,128)S(1)}, f32[19,1,8,128]{3,2,1,0:T(8,128)S(1)}, u32[]{:S(2)}, u32[]{:S(2)}) collective-permute-start(f32[19,1,8,128]{3,2,1,0:T(8,128)S(1)} %get-tuple-element.226), channel_id=1, source_target_pairs={{8,0},{16,8},{24,16},{32,24},{40,32},{48,40},{56,48},{64,56},{72,6... | collective-permute-start | bytes 233480 | tf_op jit(solution)/shard_map/ppermute | solution.py:46
  85.4 9.6 %collective-permute-start.9 = (f32[19,1,8,128]{3,2,1,0:T(8,128)S(1)}, f32[19,1,8,128]{3,2,1,0:T(8,128)S(1)}, u32[]{:S(2)}, u32[]{:S(2)}) collective-permute-start(f32[19,1,8,128]{3,2,1,0:T(8,128)S(1)} %get-tuple-element.227), channel_id=1, source_target_pairs={{0,8},{8,16},{16,24},{24,32},{32,40},{40,48},{48,56},{56,64},{64,7... | collective-permute-start | bytes 233480 | tf_op jit(solution)/shard_map/ppermute | solution.py:44
  95.1 6.1 %collective-permute-start.11 = (f32[19,6,1,128]{3,2,1,0:T(1,128)S(1)}, f32[19,6,1,128]{3,2,1,0:T(1,128)S(1)}, u32[]{:S(2)}, u32[]{:S(2)}) collective-permute-start(f32[19,6,1,128]{3,2,1,0:T(1,128)S(1)} %get-tuple-element.198), channel_id=1, source_target_pairs={{0,1},{1,2},{2,3},{3,4},{4,5},{5,6},{6,7},{7,0},{8,9},{9,10},{10,1... | collective-permute-start | bytes 175112 | tf_op jit(solution)/shard_map/ppermute | solution.py:44
  97.0 12.1 %collective-permute-start.10 = (f32[19,6,1,128]{3,2,1,0:T(1,128)S(1)}, f32[19,6,1,128]{3,2,1,0:T(1,128)S(1)}, u32[]{:S(2)}, u32[]{:S(2)}) collective-permute-start(f32[19,6,1,128]{3,2,1,0:T(1,128)S(1)} %get-tuple-element.197), channel_id=1, source_target_pairs={{1,0},{2,1},{3,2},{4,3},{5,4},{6,5},{7,6},{0,7},{9,8},{10,9},{11,1... | collective-permute-start | bytes 175112 | tf_op jit(solution)/shard_map/ppermute | solution.py:46
  101.2 9.5 %copy-start.21 = (f32[1,4,8,128]{3,2,1,0:T(8,128)}, f32[1,4,8,128]{3,2,1,0:T(8,128)S(1)}, u32[]{:S(2)}) copy-start(f32[1,4,8,128]{3,2,1,0:T(8,128)S(1)} %get-tuple-element.78) | copy-start | bytes 49156
  109.1 1.6 copy-start.23
  109.2 1.5 copy-start.25
  133.6 0.8 copy-start.1
  134.4 0.8 copy-start.2
  135.3 0.8 copy-start.3
  136.1 0.8 copy-start.4
  136.9 0.8 copy-start.5
  141.7 13.0 %all-to-all-start = ((f32[2,6,1,2,32]{1,3,2,0,4:T(2,128)}), f32[2,6,1,2,32]{1,3,2,0,4:T(2,128)S(1)}, u32[]{:S(2)}, u32[]{:S(2)}) async-start(f32[2,6,1,2,32]{1,3,2,0,4:T(2,128)} %copy.171), calls=%async_computation | async-start | bytes 131072 | tf_op jit(solution)/shard_map/all_to_all | solution.py:140
  155.6 7.8 %copy-start.38 = (f32[19]{0:T(128)S(1)}, f32[19]{0:T(128)}, u32[]{:S(2)}) copy-start(f32[19]{0:T(128)} %constant.177.clone) | copy-start | bytes 232
  157.8 5.7 %copy-start.20 = (f32[4,8,128]{2,1,0:T(8,128)S(1)}, f32[4,8,128]{2,1,0:T(8,128)}, u32[]{:S(2)}) copy-start(f32[4,8,128]{2,1,0:T(8,128)} %copy-done.19) | copy-start | bytes 49156
  157.8 15.5 %all-to-all-start.1 = ((f32[2,6,1,64]{1,0,2,3:T(2,128)}), f32[2,6,1,64]{1,0,2,3:T(2,128)S(1)}, u32[]{:S(2)}, u32[]{:S(2)}) async-start(f32[2,6,1,64]{1,0,2,3:T(2,128)} %copy.179), calls=%async_computation.1 | async-start | bytes 131072 | tf_op jit(solution)/shard_map/all_to_all | solution.py:145
  176.5 14.6 %all-to-all-start.2 = ((f32[2,3,64,1]{1,3,0,2:T(1,128)}), f32[2,3,64,1]{1,3,0,2:T(1,128)S(1)}, u32[]{:S(2)}, u32[]{:S(2)}) async-start(f32[2,3,64,1]{1,3,0,2:T(1,128)} %copy.182), calls=%async_computation.2 | async-start | bytes 131072 | tf_op jit(solution)/shard_map/all_to_all | solution.py:196
  193.0 13.5 %all-to-all-start.3 = ((f32[2,3,1,16,4]{4,0,2,1,3:T(2,128)}), f32[2,3,1,16,4]{4,0,2,1,3:T(2,128)S(1)}, u32[]{:S(2)}, u32[]{:S(2)}) async-start(f32[2,3,1,16,4]{4,0,2,1,3:T(2,128)} %copy.187), calls=%async_computation.3 | async-start | bytes 98304 | tf_op jit(solution)/shard_map/all_to_all | solution.py:199
  198.3 9.4 %collective-permute-start.13 = (f32[19,1,8,128]{3,2,1,0:T(8,128)S(1)}, f32[19,1,8,128]{3,2,1,0:T(8,128)S(1)}, u32[]{:S(2)}, u32[]{:S(2)}) collective-permute-start(f32[19,1,8,128]{3,2,1,0:T(8,128)S(1)} %get-tuple-element.222), channel_id=1, source_target_pairs={{8,0},{16,8},{24,16},{32,24},{40,32},{48,40},{56,48},{64,56},{72,6... | collective-permute-start | bytes 233480 | tf_op jit(solution)/shard_map/ppermute | solution.py:46
  200.7 9.6 %collective-permute-start.12 = (f32[19,1,8,128]{3,2,1,0:T(8,128)S(1)}, f32[19,1,8,128]{3,2,1,0:T(8,128)S(1)}, u32[]{:S(2)}, u32[]{:S(2)}) collective-permute-start(f32[19,1,8,128]{3,2,1,0:T(8,128)S(1)} %get-tuple-element.223), channel_id=1, source_target_pairs={{0,8},{8,16},{16,24},{24,32},{32,40},{40,48},{48,56},{56,64},{64,7... | collective-permute-start | bytes 233480 | tf_op jit(solution)/shard_map/ppermute | solution.py:44
  210.4 9.2 %collective-permute-start.14 = (f32[19,6,1,128]{3,2,1,0:T(1,128)S(1)}, f32[19,6,1,128]{3,2,1,0:T(1,128)S(1)}, u32[]{:S(2)}, u32[]{:S(2)}) collective-permute-start(f32[19,6,1,128]{3,2,1,0:T(1,128)S(1)} %get-tuple-element.196), channel_id=1, source_target_pairs={{0,1},{1,2},{2,3},{3,4},{4,5},{5,6},{6,7},{7,0},{8,9},{9,10},{10,1... | collective-permute-start | bytes 175112 | tf_op jit(solution)/shard_map/ppermute | solution.py:44
  217.7 12.1 %collective-permute-start.15 = (f32[19,6,1,128]{3,2,1,0:T(1,128)S(1)}, f32[19,6,1,128]{3,2,1,0:T(1,128)S(1)}, u32[]{:S(2)}, u32[]{:S(2)}) collective-permute-start(f32[19,6,1,128]{3,2,1,0:T(1,128)S(1)} %get-tuple-element.195), channel_id=1, source_target_pairs={{1,0},{2,1},{3,2},{4,3},{5,4},{6,5},{7,6},{0,7},{9,8},{10,9},{11,1... | collective-permute-start | bytes 175112 | tf_op jit(solution)/shard_map/ppermute | solution.py:46
  (27 other events, 18.9 us)
where the time goes:
time: 234 us; the launch traced here: 232 us
  waiting for transfers between devices  85.1 us (36%)
  starting transfers between devices  77.7 us (33%)
  local copies, waits for them, and re-layouts  53.3 us (23%)
  other arithmetic  8.57 us (4%)
  matrix products  4.96 us (2%)
  between operations  2.44 us (1%)
    ppermute x8, waiting for transfers between devices, with_halo(): lax.ppermute(head, axis, [((i + 1) % count, i) for i in range(count)])  35.6 us
    ppermute x8, starting transfers between devices, with_halo(): lax.ppermute(head, axis, [((i + 1) % count, i) for i in range(count)])  29.9 us
    ppermute x8, starting transfers between devices, with_halo(): lax.ppermute(tail, axis, [(i, (i + 1) % count) for i in range(count)])  27.5 us
    another operation x52, local copies, waits for them, and re-layouts, collide(): jnp.stack([moment[first] * moment[later] / density * fluid for first, lat...  26.4 us
    unnamed x172, local copies, waits for them, and re-layouts  19.1 us
    ppermute x8, waiting for transfers between devices, with_halo(): lax.ppermute(tail, axis, [(i, (i + 1) % count) for i in range(count)])  18.7 us
    all_to_all x1, waiting for transfers between devices, local(): lax.all_to_all(jnp.stack([real, imag]), 'gx', split_axis=2, concat_axis=3...  9.99 us
    all_to_all x1, waiting for transfers between devices, local(): lax.all_to_all(spectrum, 'gx', split_axis=3, concat_axis=2, tiled=True)  8.78 us
  transfers between devices with their start and end apart: 20, of which 13 were waited for; matrix products, arithmetic and copies ran while one was open for 4% of the time, Pallas kernels for 0%

commit v1 on v0

--- a/solution.py
+++ b/solution.py
@@ -193,7 +193,11 @@
         ]
     )
     real, imag = transform(speed_real, speed_imag, 1, True)
-    result = lax.all_to_all(jnp.stack([real, imag]), "gx", split_axis=2, concat_axis=3, tiled=True)
+    own = jnp.stack([real, imag])
+    devices = lax.axis_size("gx")
+    tiles = jnp.stack(jnp.split(own, devices, axis=2), axis=0)
+    tiles = lax.all_to_all(tiles, "gx", split_axis=0, concat_axis=0)
+    result = jnp.concatenate(tiles, axis=3)
     result = result.reshape(2, 3, block_x, full_y, part_z)
     real, imag = transform(result[0], result[1], 2, True)
     result = lax.all_to_all(jnp.stack([real, imag]), "gy", split_axis=3, concat_axis=4, tiled=True)

time: 234 us -> 272 us (1.16)
  local copies, waits for them, and re-layouts: 53.3 us -> 89.1 us
    unnamed x172 -> x235, local copies, waits for them, and re-layouts: 19.1 us -> 55.1 us
  transfers between devices with their start and end apart: 20 -> 20, of which waited for: 13 -> 13; matrix products, arithmetic and copies ran while one was open for 4% -> 3% of each run, Pallas kernels for 0% -> 0%
where the time goes in v1:
time: 272 us; the launch traced here: 269 us
  local copies, waits for them, and re-layouts  89.1 us (33%)
  waiting for transfers between devices  85.1 us (31%)
  starting transfers between devices  77.8 us (29%)
  other arithmetic  10 us (4%)
  matrix products  4.96 us (2%)
    unnamed x235, local copies, waits for them, and re-layouts  55.1 us
    ppermute x8, waiting for transfers between devices, with_halo(): lax.ppermute(head, axis, [((i + 1) % count, i) for i in range(count)])  35.6 us
    ppermute x8, starting transfers between devices, with_halo(): lax.ppermute(head, axis, [((i + 1) % count, i) for i in range(count)])  29.9 us
    ppermute x8, starting transfers between devices, with_halo(): lax.ppermute(tail, axis, [(i, (i + 1) % count) for i in range(count)])  27.5 us
    another operation x52, local copies, waits for them, and re-layouts, collide(): jnp.stack([moment[first] * moment[later] / density * fluid for first, lat...  26.4 us
    ppermute x8, waiting for transfers between devices, with_halo(): lax.ppermute(tail, axis, [(i, (i + 1) % count) for i in range(count)])  18.7 us
    all_to_all x1, waiting for transfers between devices, local(): tiles = lax.all_to_all(tiles, 'gx', split_axis=0, concat_axis=0)  10 us
    all_to_all x1, waiting for transfers between devices, local(): lax.all_to_all(spectrum, 'gx', split_axis=3, concat_axis=2, tiled=True)  8.79 us
  transfers between devices with their start and end apart: 20, of which 13 were waited for; matrix products, arithmetic and copies ran while one was open for 3% of the time, Pallas kernels for 0%

profile of v1, /device:TPU:6, one launch (start us, length us, event | category | flops | bytes accessed | tf_op | source)
XLA Modules:
  0.0 269.4 jit_solution(12025061787345648124)
XLA Ops:
  11.3 10.2 %collective-permute-start = (f32[19,1,8,128]{3,2,1,0:T(8,128)S(1)}, f32[19,1,8,128]{3,2,1,0:T(8,128)S(1)}, u32[]{:S(2)}, u32[]{:S(2)}) collective-permute-start(f32[19,1,8,128]{3,2,1,0:T(8,128)S(1)} %get-tuple-element.301), channel_id=1, source_target_pairs={{8,0},{16,8},{24,16},{32,24},{40,32},{48,40},{56,48},{64,56},{72,6... | collective-permute-start | bytes 233480 | tf_op jit(solution)/shard_map/ppermute | solution.py:46
  21.5 1.9 collective-permute-start.1
  28.6 2.6 collective-permute-done.1
  31.2 8.1 %collective-permute-start.3 = (f32[19,6,1,128]{3,2,1,0:T(1,128)S(1)}, f32[19,6,1,128]{3,2,1,0:T(1,128)S(1)}, u32[]{:S(2)}, u32[]{:S(2)}) collective-permute-start(f32[19,6,1,128]{3,2,1,0:T(1,128)S(1)} %get-tuple-element.269), channel_id=1, source_target_pairs={{0,1},{1,2},{2,3},{3,4},{4,5},{5,6},{6,7},{7,0},{8,9},{9,10},{10,1... | collective-permute-start | bytes 175112 | tf_op jit(solution)/shard_map/ppermute | solution.py:44
  39.4 1.9 collective-permute-start.2
  41.5 9.9 %collective-permute-done.2 = f32[19,6,1,128]{3,2,1,0:T(1,128)S(1)} collective-permute-done((f32[19,6,1,128]{3,2,1,0:T(1,128)S(1)}, f32[19,6,1,128]{3,2,1,0:T(1,128)S(1)}, u32[]{:S(2)}, u32[]{:S(2)}) %collective-permute-start.2) | collective-permute-done | bytes 58400 | tf_op jit(solution)/shard_map/ppermute | solution.py:46
  53.8 3.5 %collective-permute-start.4 = (f32[19,1,8,128]{3,2,1,0:T(8,128)S(1)}, f32[19,1,8,128]{3,2,1,0:T(8,128)S(1)}, u32[]{:S(2)}, u32[]{:S(2)}) collective-permute-start(f32[19,1,8,128]{3,2,1,0:T(8,128)S(1)} %get-tuple-element.297), channel_id=1, source_target_pairs={{8,0},{16,8},{24,16},{32,24},{40,32},{48,40},{56,48},{64,56},{72,6... | collective-permute-start | bytes 233480 | tf_op jit(solution)/shard_map/ppermute | solution.py:46
  57.3 1.9 collective-permute-start.5
  60.1 7.0 %collective-permute-done.5 = f32[19,1,8,128]{3,2,1,0:T(8,128)S(1)} collective-permute-done((f32[19,1,8,128]{3,2,1,0:T(8,128)S(1)}, f32[19,1,8,128]{3,2,1,0:T(8,128)S(1)}, u32[]{:S(2)}, u32[]{:S(2)}) %collective-permute-start.5) | collective-permute-done | bytes 77856 | tf_op jit(solution)/shard_map/ppermute | solution.py:44
  67.1 1.9 collective-permute-start.7
  69.1 3.9 %collective-permute-start.6 = (f32[19,6,1,128]{3,2,1,0:T(1,128)S(1)}, f32[19,6,1,128]{3,2,1,0:T(1,128)S(1)}, u32[]{:S(2)}, u32[]{:S(2)}) collective-permute-start(f32[19,6,1,128]{3,2,1,0:T(1,128)S(1)} %get-tuple-element.266), channel_id=1, source_target_pairs={{1,0},{2,1},{3,2},{4,3},{5,4},{6,5},{7,6},{0,7},{9,8},{10,9},{11,1... | collective-permute-start | bytes 175112 | tf_op jit(solution)/shard_map/ppermute | solution.py:46
  73.4 7.8 %collective-permute-done.6 = f32[19,6,1,128]{3,2,1,0:T(1,128)S(1)} collective-permute-done((f32[19,6,1,128]{3,2,1,0:T(1,128)S(1)}, f32[19,6,1,128]{3,2,1,0:T(1,128)S(1)}, u32[]{:S(2)}, u32[]{:S(2)}) %collective-permute-start.6) | collective-permute-done | bytes 58400 | tf_op jit(solution)/shard_map/ppermute | solution.py:46
  83.4 1.9 collective-permute-start.8
  85.4 2.4 collective-permute-start.9
  88.6 6.4 %collective-permute-done.9 = f32[19,1,8,128]{3,2,1,0:T(8,128)S(1)} collective-permute-done((f32[19,1,8,128]{3,2,1,0:T(8,128)S(1)}, f32[19,1,8,128]{3,2,1,0:T(8,128)S(1)}, u32[]{:S(2)}, u32[]{:S(2)}) %collective-permute-start.9) | collective-permute-done | bytes 77856 | tf_op jit(solution)/shard_map/ppermute | solution.py:44
  95.1 1.9 collective-permute-start.11
  97.0 4.1 %collective-permute-start.10 = (f32[19,6,1,128]{3,2,1,0:T(1,128)S(1)}, f32[19,6,1,128]{3,2,1,0:T(1,128)S(1)}, u32[]{:S(2)}, u32[]{:S(2)}) collective-permute-start(f32[19,6,1,128]{3,2,1,0:T(1,128)S(1)} %get-tuple-element.264), channel_id=1, source_target_pairs={{1,0},{2,1},{3,2},{4,3},{5,4},{6,5},{7,6},{0,7},{9,8},{10,9},{11,1... | collective-permute-start | bytes 175112 | tf_op jit(solution)/shard_map/ppermute | solution.py:46
  101.3 7.8 %collective-permute-done.10 = f32[19,6,1,128]{3,2,1,0:T(1,128)S(1)} collective-permute-done((f32[19,6,1,128]{3,2,1,0:T(1,128)S(1)}, f32[19,6,1,128]{3,2,1,0:T(1,128)S(1)}, u32[]{:S(2)}, u32[]{:S(2)}) %collective-permute-start.10) | collective-permute-done | bytes 58400 | tf_op jit(solution)/shard_map/ppermute | solution.py:46
  141.7 4.8 %all-to-all-start = ((f32[2,6,1,2,32]{1,3,2,0,4:T(2,128)}), f32[2,6,1,2,32]{1,3,2,0,4:T(2,128)S(1)}, u32[]{:S(2)}, u32[]{:S(2)}) async-start(f32[2,6,1,2,32]{1,3,2,0,4:T(2,128)} %copy.521), calls=%async_computation | async-start | bytes 131072 | tf_op jit(solution)/shard_map/all_to_all | solution.py:140
  146.5 8.2 %all-to-all-done = f32[2,6,1,2,32]{1,3,2,0,4:T(2,128)S(1)} async-done(((f32[2,6,1,2,32]{1,3,2,0,4:T(2,128)}), f32[2,6,1,2,32]{1,3,2,0,4:T(2,128)S(1)}, u32[]{:S(2)}, u32[]{:S(2)}) %all-to-all-start) | async-done | bytes 3104 | tf_op jit(solution)/shard_map/all_to_all | solution.py:140
  157.8 5.6 %all-to-all-start.1 = ((f32[2,6,1,64]{1,0,2,3:T(2,128)}), f32[2,6,1,64]{1,0,2,3:T(2,128)S(1)}, u32[]{:S(2)}, u32[]{:S(2)}) async-start(f32[2,6,1,64]{1,0,2,3:T(2,128)} %copy.529), calls=%async_computation.1 | async-start | bytes 131072 | tf_op jit(solution)/shard_map/all_to_all | solution.py:145
  164.5 8.8 %all-to-all-done.1 = f32[2,6,1,64]{1,0,2,3:T(2,128)S(1)} async-done(((f32[2,6,1,64]{1,0,2,3:T(2,128)}), f32[2,6,1,64]{1,0,2,3:T(2,128)S(1)}, u32[]{:S(2)}, u32[]{:S(2)}) %all-to-all-start.1) | async-done | bytes 3104 | tf_op jit(solution)/shard_map/all_to_all | solution.py:145
  213.8 4.6 %all-to-all-start.2 = ((f32[64,2,3,1,1]{2,1,4,3,0:T(2,128)}), f32[64,2,3,1,1]{2,1,4,3,0:T(2,128)S(1)}, u32[]{:S(2)}, u32[]{:S(2)}) async-start(f32[64,2,3,1,1]{2,1,4,3,0:T(2,128)} %constant_dynamic-update-slice_fusion.176), calls=%async_computation.2 | async-start | bytes 131072 | tf_op jit(solution)/shard_map/all_to_all | solution.py:199
  218.4 10.0 %all-to-all-done.2 = f32[64,2,3,1,1]{2,1,4,3,0:T(2,128)S(1)} async-done(((f32[64,2,3,1,1]{2,1,4,3,0:T(2,128)}), f32[64,2,3,1,1]{2,1,4,3,0:T(2,128)S(1)}, u32[]{:S(2)}, u32[]{:S(2)}) %all-to-all-start.2) | async-done | bytes 1568 | tf_op jit(solution)/shard_map/all_to_all | solution.py:199
  230.3 5.3 %all-to-all-start.3 = ((f32[2,3,1,16,4]{4,0,2,1,3:T(2,128)}), f32[2,3,1,16,4]{4,0,2,1,3:T(2,128)S(1)}, u32[]{:S(2)}, u32[]{:S(2)}) async-start(f32[2,3,1,16,4]{4,0,2,1,3:T(2,128)} %copy.536), calls=%async_computation.3 | async-start | bytes 98304 | tf_op jit(solution)/shard_map/all_to_all | solution.py:203
  235.7 2.3 collective-permute-start.13
  238.0 2.0 collective-permute-start.12
  240.0 3.8 %all-to-all-done.3 = f32[2,3,1,16,4]{4,0,2,1,3:T(2,128)S(1)} async-done(((f32[2,3,1,16,4]{4,0,2,1,3:T(2,128)}), f32[2,3,1,16,4]{4,0,2,1,3:T(2,128)S(1)}, u32[]{:S(2)}, u32[]{:S(2)}) %all-to-all-start.3) | async-done | bytes 1568 | tf_op jit(solution)/shard_map/all_to_all | solution.py:203
  245.1 2.5 collective-permute-done.12
  247.7 7.3 %collective-permute-start.14 = (f32[19,6,1,128]{3,2,1,0:T(1,128)S(1)}, f32[19,6,1,128]{3,2,1,0:T(1,128)S(1)}, u32[]{:S(2)}, u32[]{:S(2)}) collective-permute-start(f32[19,6,1,128]{3,2,1,0:T(1,128)S(1)} %get-tuple-element.263), channel_id=1, source_target_pairs={{0,1},{1,2},{2,3},{3,4},{4,5},{5,6},{6,7},{7,0},{8,9},{9,10},{10,1... | collective-permute-start | bytes 175112 | tf_op jit(solution)/shard_map/ppermute | solution.py:44
  255.0 1.9 collective-permute-start.15
  257.0 10.1 %collective-permute-done.15 = f32[19,6,1,128]{3,2,1,0:T(1,128)S(1)} collective-permute-done((f32[19,6,1,128]{3,2,1,0:T(1,128)S(1)}, f32[19,6,1,128]{3,2,1,0:T(1,128)S(1)}, u32[]{:S(2)}, u32[]{:S(2)}) %collective-permute-start.15) | collective-permute-done | bytes 58400 | tf_op jit(solution)/shard_map/ppermute | solution.py:46
  (504 shorter events, 104.3 us)
Async XLA Ops:
  0.6 7.3 %copy-start = (f32[19,4,8,128]{3,2,1,0:T(8,128)S(1)}, f32[19,4,8,128]{3,2,1,0:T(8,128)}, u32[]{:S(2)}) copy-start(f32[19,4,8,128]{3,2,1,0:T(8,128)} %param.22) | copy-start | bytes 933892
  10.2 1.1 copy-start.19
  11.3 17.2 %collective-permute-start = (f32[19,1,8,128]{3,2,1,0:T(8,128)S(1)}, f32[19,1,8,128]{3,2,1,0:T(8,128)S(1)}, u32[]{:S(2)}, u32[]{:S(2)}) collective-permute-start(f32[19,1,8,128]{3,2,1,0:T(8,128)S(1)} %get-tuple-element.301), channel_id=1, source_target_pairs={{8,0},{16,8},{24,16},{32,24},{40,32},{48,40},{56,48},{64,56},{72,6... | collective-permute-start | bytes 233480 | tf_op jit(solution)/shard_map/ppermute | solution.py:46
  21.5 9.6 %collective-permute-start.1 = (f32[19,1,8,128]{3,2,1,0:T(8,128)S(1)}, f32[19,1,8,128]{3,2,1,0:T(8,128)S(1)}, u32[]{:S(2)}, u32[]{:S(2)}) collective-permute-start(f32[19,1,8,128]{3,2,1,0:T(8,128)S(1)} %get-tuple-element.302), channel_id=1, source_target_pairs={{0,8},{8,16},{16,24},{24,32},{32,40},{40,48},{48,56},{56,64},{64,7... | collective-permute-start | bytes 233480 | tf_op jit(solution)/shard_map/ppermute | solution.py:44
  31.2 10.1 %collective-permute-start.3 = (f32[19,6,1,128]{3,2,1,0:T(1,128)S(1)}, f32[19,6,1,128]{3,2,1,0:T(1,128)S(1)}, u32[]{:S(2)}, u32[]{:S(2)}) collective-permute-start(f32[19,6,1,128]{3,2,1,0:T(1,128)S(1)} %get-tuple-element.269), channel_id=1, source_target_pairs={{0,1},{1,2},{2,3},{3,4},{4,5},{5,6},{6,7},{7,0},{8,9},{9,10},{10,1... | collective-permute-start | bytes 175112 | tf_op jit(solution)/shard_map/ppermute | solution.py:44
  39.4 12.1 %collective-permute-start.2 = (f32[19,6,1,128]{3,2,1,0:T(1,128)S(1)}, f32[19,6,1,128]{3,2,1,0:T(1,128)S(1)}, u32[]{:S(2)}, u32[]{:S(2)}) collective-permute-start(f32[19,6,1,128]{3,2,1,0:T(1,128)S(1)} %get-tuple-element.268), channel_id=1, source_target_pairs={{1,0},{2,1},{3,2},{4,3},{5,4},{6,5},{7,6},{0,7},{9,8},{10,9},{11,1... | collective-permute-start | bytes 175112 | tf_op jit(solution)/shard_map/ppermute | solution.py:46
  53.8 6.3 %collective-permute-start.4 = (f32[19,1,8,128]{3,2,1,0:T(8,128)S(1)}, f32[19,1,8,128]{3,2,1,0:T(8,128)S(1)}, u32[]{:S(2)}, u32[]{:S(2)}) collective-permute-start(f32[19,1,8,128]{3,2,1,0:T(8,128)S(1)} %get-tuple-element.297), channel_id=1, source_target_pairs={{8,0},{16,8},{24,16},{32,24},{40,32},{48,40},{56,48},{64,56},{72,6... | collective-permute-start | bytes 233480 | tf_op jit(solution)/shard_map/ppermute | solution.py:46
  57.3 9.8 %collective-permute-start.5 = (f32[19,1,8,128]{3,2,1,0:T(8,128)S(1)}, f32[19,1,8,128]{3,2,1,0:T(8,128)S(1)}, u32[]{:S(2)}, u32[]{:S(2)}) collective-permute-start(f32[19,1,8,128]{3,2,1,0:T(8,128)S(1)} %get-tuple-element.298), channel_id=1, source_target_pairs={{0,8},{8,16},{16,24},{24,32},{32,40},{40,48},{48,56},{56,64},{64,7... | collective-permute-start | bytes 233480 | tf_op jit(solution)/shard_map/ppermute | solution.py:44
  67.1 6.1 %collective-permute-start.7 = (f32[19,6,1,128]{3,2,1,0:T(1,128)S(1)}, f32[19,6,1,128]{3,2,1,0:T(1,128)S(1)}, u32[]{:S(2)}, u32[]{:S(2)}) collective-permute-start(f32[19,6,1,128]{3,2,1,0:T(1,128)S(1)} %get-tuple-element.267), channel_id=1, source_target_pairs={{0,1},{1,2},{2,3},{3,4},{4,5},{5,6},{6,7},{7,0},{8,9},{9,10},{10,1... | collective-permute-start | bytes 175112 | tf_op jit(solution)/shard_map/ppermute | solution.py:44
  69.1 12.1 %collective-permute-start.6 = (f32[19,6,1,128]{3,2,1,0:T(1,128)S(1)}, f32[19,6,1,128]{3,2,1,0:T(1,128)S(1)}, u32[]{:S(2)}, u32[]{:S(2)}) collective-permute-start(f32[19,6,1,128]{3,2,1,0:T(1,128)S(1)} %get-tuple-element.266), channel_id=1, source_target_pairs={{1,0},{2,1},{3,2},{4,3},{5,4},{6,5},{7,6},{0,7},{9,8},{10,9},{11,1... | collective-permute-start | bytes 175112 | tf_op jit(solution)/shard_map/ppermute | solution.py:46
  83.4 5.2 %collective-permute-start.8 = (f32[19,1,8,128]{3,2,1,0:T(8,128)S(1)}, f32[19,1,8,128]{3,2,1,0:T(8,128)S(1)}, u32[]{:S(2)}, u32[]{:S(2)}) collective-permute-start(f32[19,1,8,128]{3,2,1,0:T(8,128)S(1)} %get-tuple-element.293), channel_id=1, source_target_pairs={{8,0},{16,8},{24,16},{32,24},{40,32},{48,40},{56,48},{64,56},{72,6... | collective-permute-start | bytes 233480 | tf_op jit(solution)/shard_map/ppermute | solution.py:46
  85.4 9.6 %collective-permute-start.9 = (f32[19,1,8,128]{3,2,1,0:T(8,128)S(1)}, f32[19,1,8,128]{3,2,1,0:T(8,128)S(1)}, u32[]{:S(2)}, u32[]{:S(2)}) collective-permute-start(f32[19,1,8,128]{3,2,1,0:T(8,128)S(1)} %get-tuple-element.294), channel_id=1, source_target_pairs={{0,8},{8,16},{16,24},{24,32},{32,40},{40,48},{48,56},{56,64},{64,7... | collective-permute-start | bytes 233480 | tf_op jit(solution)/shard_map/ppermute | solution.py:44
  95.1 6.1 %collective-permute-start.11 = (f32[19,6,1,128]{3,2,1,0:T(1,128)S(1)}, f32[19,6,1,128]{3,2,1,0:T(1,128)S(1)}, u32[]{:S(2)}, u32[]{:S(2)}) collective-permute-start(f32[19,6,1,128]{3,2,1,0:T(1,128)S(1)} %get-tuple-element.265), channel_id=1, source_target_pairs={{0,1},{1,2},{2,3},{3,4},{4,5},{5,6},{6,7},{7,0},{8,9},{9,10},{10,1... | collective-permute-start | bytes 175112 | tf_op jit(solution)/shard_map/ppermute | solution.py:44
  97.0 12.1 %collective-permute-start.10 = (f32[19,6,1,128]{3,2,1,0:T(1,128)S(1)}, f32[19,6,1,128]{3,2,1,0:T(1,128)S(1)}, u32[]{:S(2)}, u32[]{:S(2)}) collective-permute-start(f32[19,6,1,128]{3,2,1,0:T(1,128)S(1)} %get-tuple-element.264), channel_id=1, source_target_pairs={{1,0},{2,1},{3,2},{4,3},{5,4},{6,5},{7,6},{0,7},{9,8},{10,9},{11,1... | collective-permute-start | bytes 175112 | tf_op jit(solution)/shard_map/ppermute | solution.py:46
  101.2 9.5 %copy-start.21 = (f32[1,4,8,128]{3,2,1,0:T(8,128)}, f32[1,4,8,128]{3,2,1,0:T(8,128)S(1)}, u32[]{:S(2)}) copy-start(f32[1,4,8,128]{3,2,1,0:T(8,128)S(1)} %get-tuple-element.145) | copy-start | bytes 49156
  109.1 1.6 copy-start.23
  109.2 1.5 copy-start.25
  133.5 0.8 copy-start.1
  135.2 0.8 copy-start.3
  136.0 0.8 copy-start.4
  136.9 0.8 copy-start.5
  137.7 0.8 copy-start.6
  141.7 13.0 %all-to-all-start = ((f32[2,6,1,2,32]{1,3,2,0,4:T(2,128)}), f32[2,6,1,2,32]{1,3,2,0,4:T(2,128)S(1)}, u32[]{:S(2)}, u32[]{:S(2)}) async-start(f32[2,6,1,2,32]{1,3,2,0,4:T(2,128)} %copy.521), calls=%async_computation | async-start | bytes 131072 | tf_op jit(solution)/shard_map/all_to_all | solution.py:140
  155.6 7.8 %copy-start.38 = (f32[19]{0:T(128)S(1)}, f32[19]{0:T(128)}, u32[]{:S(2)}) copy-start(f32[19]{0:T(128)} %constant.177.clone) | copy-start | bytes 232
  157.8 5.7 %copy-start.20 = (f32[4,8,128]{2,1,0:T(8,128)S(1)}, f32[4,8,128]{2,1,0:T(8,128)}, u32[]{:S(2)}) copy-start(f32[4,8,128]{2,1,0:T(8,128)} %copy-done.19) | copy-start | bytes 49156
  157.8 15.5 %all-to-all-start.1 = ((f32[2,6,1,64]{1,0,2,3:T(2,128)}), f32[2,6,1,64]{1,0,2,3:T(2,128)S(1)}, u32[]{:S(2)}, u32[]{:S(2)}) async-start(f32[2,6,1,64]{1,0,2,3:T(2,128)} %copy.529), calls=%async_computation.1 | async-start | bytes 131072 | tf_op jit(solution)/shard_map/all_to_all | solution.py:145
  213.8 14.6 %all-to-all-start.2 = ((f32[64,2,3,1,1]{2,1,4,3,0:T(2,128)}), f32[64,2,3,1,1]{2,1,4,3,0:T(2,128)S(1)}, u32[]{:S(2)}, u32[]{:S(2)}) async-start(f32[64,2,3,1,1]{2,1,4,3,0:T(2,128)} %constant_dynamic-update-slice_fusion.176), calls=%async_computation.2 | async-start | bytes 131072 | tf_op jit(solution)/shard_map/all_to_all | solution.py:199
  230.3 13.5 %all-to-all-start.3 = ((f32[2,3,1,16,4]{4,0,2,1,3:T(2,128)}), f32[2,3,1,16,4]{4,0,2,1,3:T(2,128)S(1)}, u32[]{:S(2)}, u32[]{:S(2)}) async-start(f32[2,3,1,16,4]{4,0,2,1,3:T(2,128)} %copy.536), calls=%async_computation.3 | async-start | bytes 98304 | tf_op jit(solution)/shard_map/all_to_all | solution.py:203
  235.7 9.4 %collective-permute-start.13 = (f32[19,1,8,128]{3,2,1,0:T(8,128)S(1)}, f32[19,1,8,128]{3,2,1,0:T(8,128)S(1)}, u32[]{:S(2)}, u32[]{:S(2)}) collective-permute-start(f32[19,1,8,128]{3,2,1,0:T(8,128)S(1)} %get-tuple-element.289), channel_id=1, source_target_pairs={{8,0},{16,8},{24,16},{32,24},{40,32},{48,40},{56,48},{64,56},{72,6... | collective-permute-start | bytes 233480 | tf_op jit(solution)/shard_map/ppermute | solution.py:46
  238.0 9.6 %collective-permute-start.12 = (f32[19,1,8,128]{3,2,1,0:T(8,128)S(1)}, f32[19,1,8,128]{3,2,1,0:T(8,128)S(1)}, u32[]{:S(2)}, u32[]{:S(2)}) collective-permute-start(f32[19,1,8,128]{3,2,1,0:T(8,128)S(1)} %get-tuple-element.290), channel_id=1, source_target_pairs={{0,8},{8,16},{16,24},{24,32},{32,40},{40,48},{48,56},{56,64},{64,7... | collective-permute-start | bytes 233480 | tf_op jit(solution)/shard_map/ppermute | solution.py:44
  247.7 9.2 %collective-permute-start.14 = (f32[19,6,1,128]{3,2,1,0:T(1,128)S(1)}, f32[19,6,1,128]{3,2,1,0:T(1,128)S(1)}, u32[]{:S(2)}, u32[]{:S(2)}) collective-permute-start(f32[19,6,1,128]{3,2,1,0:T(1,128)S(1)} %get-tuple-element.263), channel_id=1, source_target_pairs={{0,1},{1,2},{2,3},{3,4},{4,5},{5,6},{6,7},{7,0},{8,9},{9,10},{10,1... | collective-permute-start | bytes 175112 | tf_op jit(solution)/shard_map/ppermute | solution.py:44
  255.0 12.1 %collective-permute-start.15 = (f32[19,6,1,128]{3,2,1,0:T(1,128)S(1)}, f32[19,6,1,128]{3,2,1,0:T(1,128)S(1)}, u32[]{:S(2)}, u32[]{:S(2)}) collective-permute-start(f32[19,6,1,128]{3,2,1,0:T(1,128)S(1)} %get-tuple-element.262), channel_id=1, source_target_pairs={{1,0},{2,1},{3,2},{4,3},{5,4},{6,5},{7,6},{0,7},{9,8},{10,9},{11,1... | collective-permute-start | bytes 175112 | tf_op jit(solution)/shard_map/ppermute | solution.py:46
  (27 other events, 18.9 us)
